TPU v7x, 32 devices: a whole 2x2x4 slice. The times are simulated.
32 devices in a mesh: slab: 16 (over z, x, core), vec: 2 (over y).
Axes of the slice: x: 2, y: 2, z: 4, core: 2. Of those that a mesh axis runs over, the one named last changes fastest.
Arguments:
- block: bfloat16 [64, 3, 16, 16, 128], P('vec', None, 'slab'), may hold values from -8 to 8
- labels: int32 [16, 16, 128], P('slab'), may hold values from 0 to 3
- flags: int32 [16, 16, 128], P('slab'), may hold values 0 or 1
- stiffness: float32 [4], replicated, may hold values from 0.25 to 2.5
- density: float32 [4], replicated, may hold values from 0.5 to 4
Outputs:
- filtered: bfloat16 [64, 3, 16, 16, 128], P('vec', None, 'slab')
- gram: float32 [64, 64], P('vec')
Inputs may be any that keep to these rules, and one draw needn't show every extreme that they name: `labels`: 0 steel, 1 weld, 2 bearing, 3 void filler.
All inputs are finite; a program needn't handle non-finite values. No bound on the sum of `flags` on one device may be relied on, other than what follows from the above.
Results may differ from a plain program's by a relative error of at most 0.0049.
Values may be sent and summed in bfloat16 or wider, within the bound.
A program may use at most 64 MiB of HBM per device.

v0:
```python
import jax
import jax.numpy as jnp
from jax import lax
from jax.sharding import PartitionSpec as P

axial_modulus = 0.75
shear_modulus = 0.25
dilation_modulus = 0.5


def padded_2(block, sides, width):
    for axis, dim in sides:
        count = lax.axis_size(axis)
        forward = [(i, i + 1) for i in range(count - 1)]
        backward = [(target, source) for source, target in forward]
        low = lax.ppermute(
            lax.slice_in_dim(block, block.shape[dim] - width, None, axis=dim), axis, forward
        )
        high = lax.ppermute(lax.slice_in_dim(block, 0, width, axis=dim), axis, backward)
        block = jnp.concatenate([low, block, high], axis=dim)
    return block


def lookup_table(table, labels):
    summed = jnp.zeros(labels.shape, jnp.float32)
    for material in range(table.shape[0]):
        summed = summed + jnp.where(labels == material, table[material], jnp.float32(0.0))
    return summed


def stencil_pass(values, axis_index, operation):
    length = values.shape[axis_index] - 2
    lower = lax.slice_in_dim(values, 0, length, axis=axis_index)
    middle = lax.slice_in_dim(values, 1, length + 1, axis=axis_index)
    higher = lax.slice_in_dim(values, 2, length + 2, axis=axis_index)
    if operation == "avg":
        return (lower + 4.0 * middle + higher) / 6.0
    if operation == "second":
        return lower - 2.0 * middle + higher
    return (higher - lower) * 0.5


def separable(values, operations):
    for position in range(3):
        values = stencil_pass(values, position + 1, operations[position])
    return values


def navier(padded):
    components = [padded[:, source] for source in range(3)]
    results = []
    for target in range(3):
        summed = 0.0
        for direction in range(3):
            operations = ["avg", "avg", "avg"]
            operations[direction] = "second"
            factor = axial_modulus if direction == target else shear_modulus
            summed = summed - factor * separable(components[target], operations)
        for source in range(3):
            if source != target:
                operations = ["avg", "avg", "avg"]
                operations[target] = "first"
                operations[source] = "first"
                summed = summed - dilation_modulus * separable(components[source], operations)
        results.append(summed)
    return jnp.stack(results, axis=1)


def shards(block, labels, flags, stiffness, density):
    gain = jnp.sqrt(lookup_table(stiffness, labels)) * (1 - flags).astype(jnp.float32)
    mass = lookup_table(density, labels)
    scaled = (gain * block.astype(jnp.float32)).astype(jnp.bfloat16)
    padded = padded_2(scaled, (("slab", 2),), 1)
    padded = jnp.pad(padded.astype(jnp.float32), ((0, 0), (0, 0), (0, 0), (1, 1), (1, 1)))
    summed = navier(padded)
    filtered = (gain * summed).astype(jnp.bfloat16)
    rows_flat = filtered.reshape(
        filtered.shape[0], 3, filtered.shape[2] * filtered.shape[3], filtered.shape[4]
    )
    gathered = lax.all_to_all(rows_flat, "vec", split_axis=2, concat_axis=0, tiled=True)
    vec_count = gathered.shape[0]
    group_count = filtered.shape[0]
    share_rows = gathered.shape[2]
    mass_rows = mass.reshape(-1, mass.shape[2])
    mass_share = lax.dynamic_slice_in_dim(
        mass_rows, lax.axis_index("vec") * share_rows, share_rows, 0
    )
    weighted = (mass_share * gathered.astype(jnp.float32)).astype(jnp.bfloat16)
    partial_gram = lax.dot_general(
        gathered.reshape(vec_count, -1),
        weighted.reshape(vec_count, -1),
        (((1,), (1,)), ((), ())),
        preferred_element_type=jnp.float32,
    )
    unknowns = 3 * filtered.shape[2] * lax.axis_size("slab") * filtered.shape[3] * filtered.shape[4]
    summed_gram = lax.psum(partial_gram, ("slab", "vec"))
    row_block = lax.dynamic_slice_in_dim(
        summed_gram, lax.axis_index("vec") * group_count, group_count, 0
    )
    gram = row_block / jnp.float32(unknowns)
    return (filtered, gram)


def solution(mesh):
    in_specs = (
        P("vec", None, "slab", None, None),
        P("slab", None, None),
        P("slab", None, None),
        P(),
        P(),
    )
    out_specs = (P("vec", None, "slab", None, None), P("vec", None))
    return jax.shard_map(shards, mesh=mesh, in_specs=in_specs, out_specs=out_specs, check_vma=False)
```

profile of v0, /device:TPU:0, one launch (start us, length us, event | category | flops | bytes accessed | tf_op | source)
XLA Modules:
  0.0 80.2 jit_solution(18236181936846677165)
XLA Ops:
  0.6 1.5 %fusion.65 = (f32[1]{0:T(128)}, f32[1]{0:T(128)}, f32[1]{0:T(128)}, f32[1]{0:T(128)}) fusion(f32[4]{0:T(128)} %param.8), kind=kLoop, calls=%fused_computation.140 | loop fusion | bytes 32 | tf_op jit(solution)/shard_map/slice | solution.py:27
  2.1 3.3 %multiply_bitcast_fusion = (f32[16,128]{1,0:T(8,128)S(1)}, pred[1,16,128]{2,1,0:T(8,128)(4,1)S(1)}, pred[1,16,128]{2,1,0:T(8,128)(4,1)S(1)}, pred[1,16,128]{2,1,0:T(8,128)(4,1)S(1)}, pred[1,16,128]{2,1,0:T(8,128)(4,1)S(1)}) fusion(s32[1,16,128]{2,1,0:T(8,128)} %param.7, f32[]{:T(128)} %bitcast.3, f32[]{:T(128)} %bitcast.2, f32[]{:T(128)} %bitcast.1, ...), kind=kLoop, calls=%fused_computation.133 | loop fusion | flops 28672 | bytes 32784 | tf_op jit(solution)/shard_map/mul | solution.py:76
  5.4 1.1 %multiply_convert_fusion.1 = bf16[32,3,1,16,128]{4,0,3,2,1:T(8,128)(2,1)S(1)} fusion(bf16[32,3,1,16,128]{4,3,2,1,0:T(8,128)(2,1)} %param.5, f32[16,128]{1,0:T(8,128)S(1)} %get-tuple-element.4), kind=kLoop, calls=%fused_computation.21 | loop fusion | flops 589824 | bytes 794624 | tf_op jit(solution)/shard_map/convert_element_type | solution.py:72
  6.5 1.3 %collective-permute-start.1 = (bf16[32,3,1,16,128]{4,0,3,2,1:T(8,128)(2,1)S(1)}, bf16[32,3,1,16,128]{4,0,3,2,1:T(8,128)(2,1)S(1)}, u32[]{:S(2)}, u32[]{:S(2)}) collective-permute-start(bf16[32,3,1,16,128]{4,0,3,2,1:T(8,128)(2,1)S(1)} %multiply_convert_fusion.1), channel_id=1, source_target_pairs={{2,0},{4,2},{6,4},{8,6},{10,8},{12,10},{14,12},{16,14},{18,16},{20... | collective-permute-start | bytes 1179656 | tf_op jit(solution)/shard_map/ppermute | solution.py:19
  7.8 3.1 %collective-permute-start = (bf16[32,3,1,16,128]{4,0,3,2,1:T(8,128)(2,1)S(1)}, bf16[32,3,1,16,128]{4,0,3,2,1:T(8,128)(2,1)S(1)}, u32[]{:S(2)}, u32[]{:S(2)}) collective-permute-start(bf16[32,3,1,16,128]{4,0,3,2,1:T(8,128)(2,1)S(1)} %multiply_convert_fusion.1), channel_id=1, source_target_pairs={{0,2},{2,4},{4,6},{6,8},{8,10},{10,12},{12,14},{14,16},{16,18},{18... | collective-permute-start | bytes 1179656 | tf_op jit(solution)/shard_map/ppermute | solution.py:16
  10.8 1.5 %fusion.64 = (f32[1]{0:T(128)}, f32[1]{0:T(128)}, f32[1]{0:T(128)}, f32[1]{0:T(128)}) fusion(f32[4]{0:T(128)} %param.9), kind=kLoop, calls=%fused_computation.139 | loop fusion | bytes 32 | tf_op jit(solution)/shard_map/slice | solution.py:27
  12.3 2.6 %add_bitcast_fusion = f32[8,128]{1,0:T(8,128)S(1)} fusion(pred[1,16,128]{2,1,0:T(8,128)(4,1)S(1)} %get-tuple-element.8, s32[]{:T(128)S(6)} %select_n.39, pred[1,16,128]{2,1,0:T(8,128)(4,1)S(1)} %get-tuple-element.7, pred[1,16,128]{2,1,0:T(8,128)(4,1)S(1)} %get-tuple-element.6, pred[1,16,128]{2,1,0:T(8,128)(4,1)S(1)} %get-tuple-element.5, f32[]{:T(128)} %bitcast.20, ...), kind=kLoop, calls=%fused_computation.134 | loop fusion | flops 7168 | bytes 8212 | tf_op jit(solution)/shard_map/mul | solution.py:88
  14.9 1.7 %fusion.3 = f32[32,3,3,18,130]{4,0,3,2,1:T(8,128)S(1)} fusion(bf16[32,3,1,16,128]{4,0,3,2,1:T(8,128)(2,1)S(1)} %collective-permute-done.1, bf16[32,3,1,16,128]{4,0,3,2,1:T(8,128)(2,1)S(1)} %multiply_convert_fusion.1, bf16[32,3,1,16,128]{4,0,3,2,1:T(8,128)(2,1)S(1)} %collective-permute-done), kind=kLoop, calls=%fused_computation.8 | loop fusion | flops 12804480 | bytes 3875328 | tf_op jit(solution)/shard_map/jit(_pad)/pad | solution.py:74
  16.6 0.9 %slice_bitcast_fusion = (f32[32,3,18,130]{3,0,2,1:T(8,128)S(1)}, f32[32,3,18,130]{3,0,2,1:T(8,128)S(1)}, f32[32,3,18,130]{3,0,2,1:T(8,128)S(1)}) fusion(f32[32,3,3,18,130]{4,0,3,2,1:T(8,128)S(1)} %fusion.3), kind=kLoop, calls=%fused_computation.13 | loop fusion | bytes 5391360 | tf_op jit(solution)/shard_map/squeeze | solution.py:50
  17.4 0.5 subtract_multiply_fusion.1
  18.3 0.2 subtract_multiply_fusion.4
  18.5 0.2 subtract_add_fusion.4
  18.7 0.3 subtract_add_fusion.2
  19.2 0.2 subtract_multiply_fusion.5
  19.3 0.6 fusion.23
  20.0 0.7 fusion.37
  20.6 0.7 fusion.51
  21.3 0.8 %fusion.8 = bf16[32,3,16,128]{3,0,1,2:T(8,128)(2,1)} fusion(f32[32,1,16,128]{3,0,1,2:T(8,128)S(1)} %fusion.23, f32[32,1,16,128]{3,0,1,2:T(8,128)S(1)} %bitcast.46, f32[32,1,16,128]{3,0,1,2:T(8,128)S(1)} %bitcast.48, f32[16,128]{1,0:T(8,128)S(1)} %get-tuple-element.4), kind=kLoop, calls=%fused_computation.19 | loop fusion | flops 786432 | bytes 1187840 | tf_op jit(solution)/shard_map/convert_element_type | solution.py:76
  22.2 4.2 %all-to-all-start = ((bf16[32,3,16,128]{3,0,1,2:T(8,128)(2,1)}), bf16[32,3,16,128]{3,0,1,2:T(8,128)(2,1)S(1)}, u32[]{:S(2)}, u32[]{:S(2)}) async-start(bf16[32,3,16,128]{3,0,1,2:T(8,128)(2,1)} %fusion.8), calls=%async_computation | async-start | bytes 786432 | tf_op jit(solution)/shard_map/all_to_all | solution.py:80
  26.5 0.9 %copy.22 = bf16[32,3,1,16,128]{4,3,2,1,0:T(8,128)(2,1)} copy(bf16[32,3,1,16,128]{4,0,3,2,1:T(8,128)(2,1)S(1)} %fusion.7) | data formatting | bytes 786432
  27.4 5.1 %all-to-all-done = bf16[32,3,16,128]{3,0,1,2:T(8,128)(2,1)S(1)} async-done(((bf16[32,3,16,128]{3,0,1,2:T(8,128)(2,1)}), bf16[32,3,16,128]{3,0,1,2:T(8,128)(2,1)S(1)}, u32[]{:S(2)}, u32[]{:S(2)}) %all-to-all-start) | async-done | bytes 393248 | tf_op jit(solution)/shard_map/all_to_all | solution.py:80
  33.1 0.3 fusion.66
  33.4 46.2 %psum.7 = f32[64,64]{1,0:T(8,128)S(1)} all-reduce(f32[64,64]{1,0:T(8,128)S(1)} %fusion.66), channel_id=1, replica_groups=mesh['slab'=16,'vec'=2] {'slab','vec'}, use_global_device_ids=true, to_apply=%region_0.1 | all-reduce | flops 4096 | bytes 32768 | tf_op jit(solution)/shard_map/psum | solution.py:96
  79.6 0.6 dynamic-slice_multiply_fusion
  (12 shorter events, 1.2 us)
Async XLA Ops:
  6.5 8.4 %collective-permute-start.1 = (bf16[32,3,1,16,128]{4,0,3,2,1:T(8,128)(2,1)S(1)}, bf16[32,3,1,16,128]{4,0,3,2,1:T(8,128)(2,1)S(1)}, u32[]{:S(2)}, u32[]{:S(2)}) collective-permute-start(bf16[32,3,1,16,128]{4,0,3,2,1:T(8,128)(2,1)S(1)} %multiply_convert_fusion.1), channel_id=1, source_target_pairs={{2,0},{4,2},{6,4},{8,6},{10,8},{12,10},{14,12},{16,14},{18,16},{20... | collective-permute-start | bytes 1179656 | tf_op jit(solution)/shard_map/ppermute | solution.py:19
  7.8 7.1 %collective-permute-start = (bf16[32,3,1,16,128]{4,0,3,2,1:T(8,128)(2,1)S(1)}, bf16[32,3,1,16,128]{4,0,3,2,1:T(8,128)(2,1)S(1)}, u32[]{:S(2)}, u32[]{:S(2)}) collective-permute-start(bf16[32,3,1,16,128]{4,0,3,2,1:T(8,128)(2,1)S(1)} %multiply_convert_fusion.1), channel_id=1, source_target_pairs={{0,2},{2,4},{4,6},{6,8},{8,10},{10,12},{12,14},{14,16},{16,18},{18... | collective-permute-start | bytes 1179656 | tf_op jit(solution)/shard_map/ppermute | solution.py:16
  22.2 10.3 %all-to-all-start = ((bf16[32,3,16,128]{3,0,1,2:T(8,128)(2,1)}), bf16[32,3,16,128]{3,0,1,2:T(8,128)(2,1)S(1)}, u32[]{:S(2)}, u32[]{:S(2)}) async-start(bf16[32,3,16,128]{3,0,1,2:T(8,128)(2,1)} %fusion.8), calls=%async_computation | async-start | bytes 786432 | tf_op jit(solution)/shard_map/all_to_all | solution.py:80
where the time goes:
time: 80.7 us; the launch traced here: 80.2 us
  blocking collectives  46.2 us (57%)
  other arithmetic  14.1 us (17%)
  starting transfers between devices  8.58 us (11%)
  local copies, waits for them, and re-layouts  5.18 us (6%)
  waiting for transfers between devices  5.07 us (6%)
  between operations  0.83 us (1%)
    psum x1, blocking collectives, shards(): summed_gram = lax.psum(partial_gram, ('slab', 'vec'))  46.2 us
    all_to_all x1, waiting for transfers between devices, shards(): lax.all_to_all(rows_flat, 'vec', split_axis=2, concat_axis=0, tiled=True)  5.06 us
    all_to_all x1, starting transfers between devices, shards(): lax.all_to_all(rows_flat, 'vec', split_axis=2, concat_axis=0, tiled=True)  4.23 us
    mul x1, other arithmetic, shards(): filtered = (gain * summed).astype(jnp.bfloat16)  3.28 us
    ppermute x1, starting transfers between devices, padded_2(): lax.ppermute(lax.slice_in_dim(block, block.shape[dim] - width, None, axis...  3.05 us
    slice x2, local copies, waits for them, and re-layouts, lookup_table(): table[material]  2.92 us
    mul x1, other arithmetic, shards(): weighted = (mass_share * gathered.astype(jnp.float32)).astype(jnp.bfloat16)  2.56 us
    sub x3, other arithmetic, navier(): summed - dilation_modulus * separable(components[source], operations)  1.99 us
  transfers between devices with their start and end apart: 3, of which 1 were waited for; matrix products, arithmetic and copies ran while one was open for 6% of the time, Pallas kernels for 0%

commit v1 on v0

v1 whole, which is shorter than its diff:
```python
import functools

import jax
import jax.numpy as jnp
from jax import lax
from jax.experimental import pallas as pl
from jax.experimental.pallas import tpu as pltpu
from jax.sharding import PartitionSpec as P

MESH = pl.DeviceIdType.MESH
CHUNKS = 4

A = (1, 4, 1)
S = (1, -2, 1)
D = (-1, 0, 1)
TERMS = (
    (((3, S, A), (1, A, S)), ((1, A, A),), ((3, D, A),), ((3, D, D),)),
    (((3, D, A),), ((1, S, A), (1, A, S)), ((3, A, A),), ((3, A, D),)),
    (((3, D, D),), ((3, A, D),), ((1, S, A), (3, A, S)), ((1, A, A),)),
)


def lookup(table_ref, labels):
    summed = jnp.zeros(labels.shape, jnp.float32)
    for material in range(table_ref.shape[0]):
        summed = summed + jnp.where(labels == material, table_ref[material], jnp.float32(0.0))
    return summed


def kernel(
    slabs, groups, inner, unknowns,
    block, labels_ref, flags_ref, stiff_ref, dens_ref,
    out, gram_out,
    raw, planes, weights, filt, own_w, pairs, near, far,
    in_sem, hs, hr, vs, vr, out_sem, ns, nr, fs, fr,
):
    vecs, comps, ny, nz = raw.shape
    per = vecs // CHUNKS
    outer = slabs // inner
    me = lax.axis_index("slab")
    mine = lax.axis_index("vec")
    ii, oi = lax.rem(me, inner), me // inner
    near_ids = [oi * inner + lax.rem(ii + r, inner) for r in range(1, inner)]
    far_ids = [lax.rem(oi + r, outer) * inner + ii for r in range(1, outer)]
    vec_ids = [lax.rem(mine + r, groups) for r in range(1, groups)]

    loads = [
        pltpu.make_async_copy(
            block.at[pl.ds(k * per, per)], raw.at[pl.ds(k * per, per)], in_sem.at[k]
        )
        for k in range(CHUNKS)
    ]
    for copy in loads:
        copy.start()

    barrier = pltpu.get_barrier_semaphore()

    @pl.when(me > 0)
    def _():
        pl.semaphore_signal(barrier, inc=1, device_id=(me - 1, mine), device_id_type=MESH)

    @pl.when(me < slabs - 1)
    def _():
        pl.semaphore_signal(barrier, inc=1, device_id=(me + 1, mine), device_id_type=MESH)

    for peer in near_ids + far_ids:
        pl.semaphore_signal(barrier, inc=1, device_id=(peer, mine), device_id_type=MESH)
    for peer in vec_ids:
        pl.semaphore_signal(barrier, inc=1, device_id=(me, peer), device_id_type=MESH)

    labels = labels_ref[0]
    gain = jnp.sqrt(lookup(stiff_ref, labels)) * (1 - flags_ref[0]).astype(jnp.float32)
    mass = lookup(dens_ref, labels)

    for k in range(CHUNKS):
        part = pl.ds(k * per, per)
        loads[k].wait()
        planes[1, part] = (gain * raw[part].astype(jnp.float32)).astype(jnp.bfloat16)

    @pl.when(me == 0)
    def _():
        planes[0] = jnp.zeros_like(planes[0])

    @pl.when(me == slabs - 1)
    def _():
        planes[2] = jnp.zeros_like(planes[2])

    pl.semaphore_wait(
        barrier,
        len(near_ids + far_ids + vec_ids)
        + jnp.where(me > 0, 1, 0) + jnp.where(me < slabs - 1, 1, 0),
    )

    def halo(k, up):
        part = pl.ds(k * per, per)
        return pltpu.make_async_remote_copy(
            src_ref=planes.at[1, part],
            dst_ref=planes.at[0 if up else 2, part],
            send_sem=hs.at[up, k],
            recv_sem=hr.at[up, k],
            device_id=(me + 1 if up else me - 1, mine),
            device_id_type=MESH,
        )

    for k in range(CHUNKS):
        @pl.when(me < slabs - 1)
        def _():
            halo(k, 1).start()

        @pl.when(me > 0)
        def _():
            halo(k, 0).start()

    offset = (
        lax.broadcasted_iota(jnp.int32, (nz, nz), 0)
        - lax.broadcasted_iota(jnp.int32, (nz, nz), 1)
    )
    low, middle, high = offset == -1, offset == 0, offset == 1
    for source in range(3):
        for position, terms in enumerate(TERMS[source]):
            for plane in range(3):
                tap = [float(sum(f * x[plane] * y[t] for f, x, y in terms)) for t in range(3)]
                tile = jnp.where(low, tap[0], jnp.where(middle, tap[1], jnp.where(high, tap[2], 0.0)))
                weights[source, plane * nz:(plane + 1) * nz, position * nz:(position + 1) * nz] = (
                    tile.astype(jnp.bfloat16)
                )

    rows = per * ny
    row = lax.rem(lax.broadcasted_iota(jnp.int32, (rows, nz), 0), ny)
    first_row, last_row = row == 0, row == ny - 1
    factor = jnp.tile(gain * jnp.float32(-1.0 / 144.0), (per, 1))
    mass_rows = jnp.tile(mass, (per, 1))
    same = row == lax.rem(lax.broadcasted_iota(jnp.int32, (rows, rows), 1), ny)

    def flat(ref, part):
        return jnp.concatenate([ref[part, c].reshape(-1, nz) for c in range(3)], axis=-1)

    def pair(a, group, b):
        product = lax.dot_general(
            flat(own_w, pl.ds(a * per, per)),
            flat(filt.at[group], pl.ds(b * per, per)),
            (((1,), (1,)), ((), ())),
            preferred_element_type=jnp.float32,
        )
        kept = jnp.where(same, product, 0.0).reshape(per, ny, rows)
        pairs[group, a * per:(a + 1) * per, b * rows:(b + 1) * rows] = jnp.sum(kept, axis=1)

    def corner(group, k):
        for a in range(k + 1):
            pair(a, group, k)
        for b in range(k):
            pair(k, group, b)

    def share(k, r):
        part = pl.ds(k * per, per)
        return pltpu.make_async_remote_copy(
            src_ref=filt.at[mine, part],
            dst_ref=filt.at[mine, part],
            send_sem=vs.at[r - 1, k],
            recv_sem=vr.at[r - 1, k],
            device_id=(me, vec_ids[r - 1]),
            device_id_type=MESH,
        )

    def store(k):
        part = pl.ds(k * per, per)
        return pltpu.make_async_copy(filt.at[mine, part], out.at[part], out_sem.at[k])

    def others(k):
        for r in range(1, groups):
            share(k, r).wait_recv()
            corner(lax.rem(mine + groups - r, groups), k)

    for k in range(CHUNKS):
        part = pl.ds(k * per, per)

        @pl.when(me > 0)
        def _():
            halo(k, 1).wait_recv()

        @pl.when(me < slabs - 1)
        def _():
            halo(k, 0).wait_recv()

        passed = []
        for source in range(3):
            data = jnp.concatenate(
                [planes[p, part, source].reshape(rows, nz) for p in range(3)], axis=-1
            )
            passed.append(
                jnp.dot(data, weights[source], preferred_element_type=jnp.float32)
            )
        piece = lambda source, position: passed[source][:, position * nz:(position + 1) * nz]
        x = [piece(0, 0) + piece(2, 0), piece(1, 1), piece(0, 3) + piece(2, 2)]
        y = [piece(0, 1), piece(1, 2), piece(2, 3)]
        z = [piece(1, 0), piece(0, 2) + piece(2, 1), piece(1, 3)]
        for c in range(3):
            both = x[c] + y[c]
            before = jnp.where(first_row, 0.0, pltpu.roll(both - z[c], 1, 0))
            after = jnp.where(last_row, 0.0, pltpu.roll(both + z[c], rows - 1, 0))
            value = factor * (4.0 * x[c] - 2.0 * y[c] + before + after)
            value = value.astype(jnp.bfloat16)
            filt[mine, part, c] = value.reshape(per, ny, nz)
            heavy = (mass_rows * value.astype(jnp.float32)).astype(jnp.bfloat16)
            own_w[part, c] = heavy.reshape(per, ny, nz)
        for r in range(1, groups):
            share(k, r).start()
        store(k).start()
        corner(mine, k)
        if k > 0:
            others(k - 1)
    others(CHUNKS - 1)

    total_cols = groups * vecs
    fold = max(1, 128 // total_cols)
    wide = fold * total_cols
    height = vecs // fold
    gram = jnp.zeros((vecs, wide), jnp.float32)
    depth = vecs * ny
    vector = lax.broadcasted_iota(jnp.int32, (depth, wide), 0) // ny
    column = lax.rem(lax.broadcasted_iota(jnp.int32, (depth, wide), 1), total_cols)
    for group in range(groups):
        select = jnp.where(vector + group * vecs == column, 1.0, 0.0)
        gram = gram + jnp.dot(
            pairs[group], select,
            preferred_element_type=jnp.float32, precision=lax.Precision.HIGHEST,
        )
    packed = gram[:height]
    lane = lax.broadcasted_iota(jnp.int32, (height, wide), 1) // total_cols
    for f in range(1, fold):
        packed = jnp.where(lane == f, gram[f * height:(f + 1) * height], packed)

    def exchange(buffer, index, count, ids, send, recv, value):
        buffer[index] = value
        copies = [
            pltpu.make_async_remote_copy(
                src_ref=buffer.at[index],
                dst_ref=buffer.at[index],
                send_sem=send.at[r],
                recv_sem=recv.at[r],
                device_id=(ids[r], mine),
                device_id_type=MESH,
            )
            for r in range(count - 1)
        ]
        for copy in copies:
            copy.start()
        for copy in copies:
            copy.wait_recv()
        summed = buffer[0]
        for slot in range(1, count):
            summed = summed + buffer[slot]
        return summed, copies

    summed, near_copies = exchange(near, ii, inner, near_ids, ns, nr, packed)
    summed, far_copies = exchange(far, oi, outer, far_ids, fs, fr, summed)
    summed = summed / jnp.float32(unknowns)
    for f in range(fold):
        gram_out[f * height:(f + 1) * height, :] = summed[:, f * total_cols:(f + 1) * total_cols]

    for k in range(CHUNKS):
        @pl.when(me < slabs - 1)
        def _():
            halo(k, 1).wait_send()

        @pl.when(me > 0)
        def _():
            halo(k, 0).wait_send()

        for r in range(1, groups):
            share(k, r).wait_send()
        store(k).wait()
    for copy in near_copies + far_copies:
        copy.wait_send()


def shards(block, labels, flags, stiffness, density):
    slabs, groups = lax.axis_size("slab"), lax.axis_size("vec")
    vecs, comps, _, ny, nz = block.shape
    inner = 1
    while inner * inner < slabs:
        inner *= 2
    outer = slabs // inner
    total_cols = groups * vecs
    fold = max(1, 128 // total_cols)
    flat_block = block.reshape(vecs, comps, ny, nz)
    bf16, f32 = jnp.bfloat16, jnp.float32
    dma = pltpu.SemaphoreType.DMA
    vmem = pl.BlockSpec(memory_space=pltpu.VMEM)
    smem = pl.BlockSpec(memory_space=pltpu.SMEM)
    anywhere = pl.BlockSpec(memory_space=pl.ANY)
    filtered, gram = pl.pallas_call(
        functools.partial(kernel, slabs, groups, inner, comps * slabs * ny * nz),
        out_shape=(
            jax.ShapeDtypeStruct((vecs, comps, ny, nz), bf16),
            jax.ShapeDtypeStruct((vecs, total_cols), f32),
        ),
        in_specs=[anywhere, vmem, vmem, smem, smem],
        out_specs=(anywhere, vmem),
        scratch_shapes=[
            pltpu.VMEM((vecs, comps, ny, nz), bf16),
            pltpu.VMEM((3, vecs, comps, ny, nz), bf16),
            pltpu.VMEM((3, 3 * nz, 4 * nz), bf16),
            pltpu.VMEM((groups, vecs, comps, ny, nz), bf16),
            pltpu.VMEM((vecs, comps, ny, nz), bf16),
            pltpu.VMEM((groups, vecs, vecs * ny), f32),
            pltpu.VMEM((inner, vecs // fold, fold * total_cols), f32),
            pltpu.VMEM((outer, vecs // fold, fold * total_cols), f32),
            dma((CHUNKS,)),
            dma((2, CHUNKS)),
            dma((2, CHUNKS)),
            dma((groups - 1, CHUNKS)),
            dma((groups - 1, CHUNKS)),
            dma((CHUNKS,)),
            dma((inner - 1,)),
            dma((inner - 1,)),
            dma((outer - 1,)),
            dma((outer - 1,)),
        ],
        compiler_params=pltpu.CompilerParams(collective_id=0, has_side_effects=True),
        name="stiffness_gram",
    )(flat_block, labels, flags, stiffness, density)
    return filtered.reshape(block.shape), gram


def solution(mesh):
    in_specs = (
        P("vec", None, "slab", None, None),
        P("slab", None, None),
        P("slab", None, None),
        P(),
        P(),
    )
    out_specs = (P("vec", None, "slab", None, None), P("vec", None))
    return jax.shard_map(shards, mesh=mesh, in_specs=in_specs, out_specs=out_specs, check_vma=False)
```

time: 80.7 us -> 33.6 us (0.42)
  blocking collectives: 46.2 us -> 0 us
  Pallas kernels: 0 us -> 30.3 us
  other arithmetic: 14.1 us -> 0 us
  starting transfers between devices: 8.58 us -> 0 us
  waiting for transfers between devices: 5.07 us -> 0 us
  local copies, waits for them, and re-layouts: 5.18 us -> 2.38 us
    psum x1 -> x0, blocking collectives: 46.2 us -> none  [shards(): summed_gram = lax.psum(partial_gram, ('slab', 'vec'))]
    pallas_call x0 -> x1, Pallas kernels: none -> 30.3 us  [shards(): pl.pallas_call(functools.partial(kernel, slabs, groups, inner, comps * sl...]
    mul x6 -> x0, other arithmetic: 6.79 us -> none  [the longest x1 3.28 us: shards(): filtered = (gain * summed).astype(jnp.bfloat16)]
    all_to_all x1 -> x0, waiting for transfers between devices: 5.06 us -> none  [shards(): lax.all_to_all(rows_flat, 'vec', split_axis=2, concat_axis=0, tiled=True)]
    ppermute x2 -> x0, starting transfers between devices: 4.35 us -> none  [the longest x1 3.05 us: padded_2(): lax.ppermute(lax.slice_in_dim(block, block.shape[dim] - width, None, axis...]
    all_to_all x1 -> x0, starting transfers between devices: 4.23 us -> none  [shards(): lax.all_to_all(rows_flat, 'vec', split_axis=2, concat_axis=0, tiled=True)]
    slice x2 -> x0, local copies, waits for them, and re-layouts: 2.92 us -> none  [lookup_table(): table[material]]
    convert_element_type x4 -> x0, other arithmetic: 2.16 us -> none  [the longest x1 1.11 us: shards(): scaled = (gain * block.astype(jnp.float32)).astype(jnp.bfloat16)]
  transfers between devices with their start and end apart: 3 -> 0, of which waited for: 1 -> 0; matrix products, arithmetic and copies ran while one was open for 6% -> 0% of each run, Pallas kernels for 0% -> 0%
where the time goes in v1:
time: 33.6 us; the launch traced here: 33.4 us
  Pallas kernels  30.3 us (90%)
  local copies, waits for them, and re-layouts  2.38 us (7%)
  between operations  0.65 us (2%)
    pallas_call x1, Pallas kernels, shards(): pl.pallas_call(functools.partial(kernel, slabs, groups, inner, comps * sl...  30.3 us
    unnamed x4, local copies, waits for them, and re-layouts  2.38 us

profile of v1, /device:TPU:0, one launch (start us, length us, event | category | flops | bytes accessed | tf_op | source)
XLA Modules:
  0.0 33.4 jit_solution(6645832585179674817)
XLA Ops:
  0.6 30.3 %stiffness_gram.1 = (bf16[32,3,16,128]{3,2,1,0:T(8,128)(2,1)}, f32[32,64]{1,0:T(8,128)}) custom-call(bf16[32,3,16,128]{3,2,1,0:T(8,128)(2,1)} %bitcast.4, s32[1,16,128]{2,1,0:T(8,128)} %labels_ref.1, s32[1,16,128]{2,1,0:T(8,128)} %flags_ref.1, f32[4]{0:T(128)} %stiff_ref.1, f32[4]{0:T(128)} %dens_ref.1), custom_call_target="tpu_custom_call" | custom-call | tf_op jit(solution)/shard_map/stiffness_gram/pallas_call | solution.py:292
  31.0 0.0 copy-start
  31.0 1.8 %copy.10 = bf16[32,3,1,16,128]{4,3,2,1,0:T(8,128)(2,1)} copy(bf16[32,3,1,16,128]{4,3,2,1,0:T(8,128)(2,1)} %bitcast.5) | data formatting | bytes 786432
  32.8 0.0 copy-done
  32.8 0.6 %copy.11 = f32[32,64]{1,0:T(8,128)} copy(f32[32,64]{1,0:T(8,128)S(1)} %copy-done) | data formatting | bytes 16384
Async XLA Ops:
  31.0 1.8 %copy-start = (f32[32,64]{1,0:T(8,128)S(1)}, f32[32,64]{1,0:T(8,128)}, u32[]{:S(2)}) copy-start(f32[32,64]{1,0:T(8,128)} %get-tuple-element.11) | copy-start | bytes 24580

commit v2 on v1

v2 whole, which is shorter than its diff:
```python
import functools

import jax
import jax.numpy as jnp
from jax import lax
from jax.experimental import pallas as pl
from jax.experimental.pallas import tpu as pltpu
from jax.sharding import PartitionSpec as P

MESH = pl.DeviceIdType.MESH
SIZES = (8, 8, 8, 4, 4)
UNIT = 8

A = (1, 4, 1)
S = (1, -2, 1)
D = (-1, 0, 1)
TERMS = (
    (((3, S, A), (1, A, S)), ((1, A, A),), ((3, D, A),), ((3, D, D),)),
    (((3, D, A),), ((1, S, A), (1, A, S)), ((3, A, A),), ((3, A, D),)),
    (((3, D, D),), ((3, A, D),), ((1, S, A), (3, A, S)), ((1, A, A),)),
)


def lookup(table_ref, labels):
    summed = jnp.zeros(labels.shape, jnp.float32)
    for material in range(table_ref.shape[0]):
        summed = summed + jnp.where(labels == material, table_ref[material], jnp.float32(0.0))
    return summed


def kernel(
    slabs, groups, inner, unknowns,
    block, labels_hbm, flags_hbm, stiff_hbm, dens_hbm,
    out, gram_out,
    raw, labels_ref, flags_ref, stiff_ref, dens_ref,
    planes, weights, shared, taken, heavy, pairs, grams, near, far,
    in_sem, hs, hr, vs, vr, ns, nr, fs, fr,
):
    vecs, comps, ny, nz = raw.shape
    cuts, part_rows = shared.shape[0], shared.shape[3]
    outer = slabs // inner
    me = lax.axis_index("slab")
    mine = lax.axis_index("vec")
    own_cut = mine if cuts > 1 else 0
    ii, oi = lax.rem(me, inner), me // inner
    vec_ids = [lax.rem(mine + r, groups) for r in range(groups)]
    near_ids = [
        (oi * inner + lax.rem(ii + r, inner), vec_ids[q])
        for q in range(cuts) for r in range(inner) if q or r
    ]
    far_ids = [(lax.rem(oi + r, outer) * inner + ii, mine) for r in range(1, outer)]
    peers = near_ids + far_ids + [(me, vec_ids[q]) for q in range(1, groups) if cuts == 1]

    barrier = pltpu.get_barrier_semaphore()

    @pl.when(me > 0)
    def _():
        pl.semaphore_signal(barrier, inc=1, device_id=(me - 1, mine), device_id_type=MESH)

    @pl.when(me < slabs - 1)
    def _():
        pl.semaphore_signal(barrier, inc=1, device_id=(me + 1, mine), device_id_type=MESH)

    for peer in peers:
        pl.semaphore_signal(barrier, inc=1, device_id=peer, device_id_type=MESH)

    tables = [
        pltpu.make_async_copy(source, target, in_sem.at[k])
        for k, (source, target) in enumerate(
            ((labels_hbm.at[0], labels_ref), (flags_hbm.at[0], flags_ref),
             (stiff_hbm, stiff_ref), (dens_hbm, dens_ref))
        )
    ]
    load = pltpu.make_async_copy(block, raw, in_sem.at[4])
    for copy in tables:
        copy.start()
    load.start()

    @pl.when(me == 0)
    def _():
        planes[0] = jnp.zeros_like(planes[0])

    @pl.when(me == slabs - 1)
    def _():
        planes[2] = jnp.zeros_like(planes[2])

    for copy in tables:
        copy.wait()
    labels = labels_ref[...]
    gain = jnp.sqrt(lookup(stiff_ref, labels)) * (1 - flags_ref[...]).astype(jnp.float32)
    mass = lookup(dens_ref, labels)
    load.wait()
    planes[1] = (gain * raw[...].astype(jnp.float32)).astype(jnp.bfloat16)

    pl.semaphore_wait(
        barrier, len(peers) + jnp.where(me > 0, 1, 0) + jnp.where(me < slabs - 1, 1, 0)
    )

    starts = [sum(SIZES[:k]) for k in range(len(SIZES))]
    parts = [pl.ds(start, size) for start, size in zip(starts, SIZES)]

    def halo(k, up):
        return pltpu.make_async_remote_copy(
            src_ref=planes.at[1, parts[k]],
            dst_ref=planes.at[0 if up else 2, parts[k]],
            send_sem=hs.at[up, k],
            recv_sem=hr.at[up, k],
            device_id=(me + 1 if up else me - 1, mine),
            device_id_type=MESH,
        )

    for k in range(len(SIZES)):
        @pl.when(me < slabs - 1)
        def _():
            halo(k, 1).start()

        @pl.when(me > 0)
        def _():
            halo(k, 0).start()

    offset = (
        lax.broadcasted_iota(jnp.int32, (nz, nz), 0)
        - lax.broadcasted_iota(jnp.int32, (nz, nz), 1)
    )
    low, middle, high = offset == -1, offset == 0, offset == 1
    for source in range(3):
        for position, terms in enumerate(TERMS[source]):
            for plane in range(3):
                tap = [float(sum(f * x[plane] * y[t] for f, x, y in terms)) for t in range(3)]
                tile = jnp.where(low, tap[0], jnp.where(middle, tap[1], jnp.where(high, tap[2], 0.0)))
                weights[source, plane * nz:(plane + 1) * nz, position * nz:(position + 1) * nz] = (
                    tile.astype(jnp.bfloat16)
                )

    scale = gain * jnp.float32(-1.0 / 144.0)
    if cuts > 1:
        own_mass = mass[:part_rows]
        for cut in range(1, cuts):
            own_mass = jnp.where(mine == cut, mass[cut * part_rows:(cut + 1) * part_rows], own_mass)
    else:
        own_mass = mass

    unit_rows = UNIT * part_rows
    same = (
        lax.rem(lax.broadcasted_iota(jnp.int32, (unit_rows, unit_rows), 0), part_rows)
        == lax.rem(lax.broadcasted_iota(jnp.int32, (unit_rows, unit_rows), 1), part_rows)
    )

    def flat(ref, unit):
        part = pl.ds(unit * UNIT, UNIT)
        return jnp.concatenate([ref[part, c].reshape(-1, nz) for c in range(3)], axis=-1)

    held = lambda r: taken.at[r - 1] if r else shared.at[own_cut]

    def pair(r, a, q, b):
        product = lax.dot_general(
            flat(heavy.at[r], a), flat(held(q), b),
            (((1,), (1,)), ((), ())),
            preferred_element_type=jnp.float32,
        )
        kept = jnp.where(same, product, 0.0).reshape(UNIT, part_rows, unit_rows)
        pairs[
            r, vec_ids[q], a * UNIT:(a + 1) * UNIT, b * unit_rows:(b + 1) * unit_rows
        ] = jnp.sum(kept, axis=1)

    done = []

    def corner(r, unit):
        done.append((r, unit))
        for q, b in done:
            if r == 0 or cuts > 1:
                pair(r, unit, q, b)
            if (q, b) != (r, unit) and (q == 0 or cuts > 1):
                pair(q, b, r, unit)

    def weigh(r, start, size):
        part = pl.ds(start, size)
        heavy[r, part] = (own_mass * held(r)[part].astype(jnp.float32)).astype(jnp.bfloat16)

    def share(k, r):
        cut = vec_ids[r] if cuts > 1 else 0
        return pltpu.make_async_remote_copy(
            src_ref=shared.at[cut, parts[k]],
            dst_ref=taken.at[groups - r - 1, parts[k]],
            send_sem=vs.at[r - 1, k],
            recv_sem=vr.at[groups - r - 1, k],
            device_id=(me, vec_ids[r]),
            device_id_type=MESH,
        )

    def arrived(k, r):
        return pltpu.make_async_remote_copy(
            src_ref=taken.at[r - 1, parts[k]],
            dst_ref=taken.at[r - 1, parts[k]],
            send_sem=vs.at[r - 1, k],
            recv_sem=vr.at[r - 1, k],
            device_id=(me, vec_ids[r]),
            device_id_type=MESH,
        )

    def others(k):
        for r in range(1, groups):
            arrived(k, r).wait_recv()
            if cuts > 1:
                weigh(r, starts[k], SIZES[k])
            if (starts[k] + SIZES[k]) % UNIT == 0:
                corner(r, starts[k] // UNIT)

    for k, size in enumerate(SIZES):
        part = parts[k]
        rows = size * ny
        row = lax.rem(lax.broadcasted_iota(jnp.int32, (rows, nz), 0), ny)
        first_row, last_row = row == 0, row == ny - 1
        factor = jnp.tile(scale, (size, 1))

        @pl.when(me > 0)
        def _():
            halo(k, 1).wait_recv()

        @pl.when(me < slabs - 1)
        def _():
            halo(k, 0).wait_recv()

        passed = []
        for source in range(3):
            data = jnp.concatenate(
                [planes[p, part, source].reshape(rows, nz) for p in range(3)], axis=-1
            )
            passed.append(
                jnp.dot(data, weights[source], preferred_element_type=jnp.float32)
            )
        piece = lambda source, position: passed[source][:, position * nz:(position + 1) * nz]
        x = [piece(0, 0) + piece(2, 0), piece(1, 1), piece(0, 3) + piece(2, 2)]
        y = [piece(0, 1), piece(1, 2), piece(2, 3)]
        z = [piece(1, 0), piece(0, 2) + piece(2, 1), piece(1, 3)]
        for c in range(3):
            both = x[c] + y[c]
            before = jnp.where(first_row, 0.0, pltpu.roll(both - z[c], 1, 0))
            after = jnp.where(last_row, 0.0, pltpu.roll(both + z[c], rows - 1, 0))
            value = factor * (4.0 * x[c] - 2.0 * y[c] + before + after)
            value = value.reshape(size, ny, nz)
            for cut in range(cuts):
                shared[cut, part, c] = (
                    value[:, cut * part_rows:(cut + 1) * part_rows].astype(jnp.bfloat16)
                )
            out[part, c] = value.astype(jnp.bfloat16)
        for r in range(1, groups):
            share(k, r).start()
        weigh(0, starts[k], size)
        if (starts[k] + size) % UNIT == 0:
            corner(0, starts[k] // UNIT)
        if k > 0:
            others(k - 1)
    others(len(SIZES) - 1)

    total_cols = groups * vecs
    fold = max(1, 128 // total_cols)
    wide = fold * total_cols
    height = vecs // fold
    depth = vecs * part_rows
    vector = lax.broadcasted_iota(jnp.int32, (depth, wide), 0) // part_rows
    column = lax.rem(lax.broadcasted_iota(jnp.int32, (depth, wide), 1), total_cols)
    lane = lax.broadcasted_iota(jnp.int32, (height, wide), 1) // total_cols
    total = jnp.zeros((cuts * vecs, wide), jnp.float32)
    for group in range(groups):
        select = jnp.where(vector + group * vecs == column, 1.0, 0.0)
        total = total + jnp.dot(
            pairs[:, group].reshape(cuts * vecs, depth), select,
            preferred_element_type=jnp.float32, precision=lax.Precision.HIGHEST,
        )
    for q in range(cuts):
        packed = total[q * vecs:q * vecs + height]
        for f in range(1, fold):
            packed = jnp.where(
                lane == f, total[q * vecs + f * height:q * vecs + (f + 1) * height], packed
            )
        grams[q] = packed

    def exchange(buffer, slot, ids, sources, send, recv):
        copies = [
            pltpu.make_async_remote_copy(
                src_ref=sources[r],
                dst_ref=buffer.at[slot],
                send_sem=send.at[r],
                recv_sem=recv.at[r],
                device_id=ids[r],
                device_id_type=MESH,
            )
            for r in range(len(ids))
        ]
        for copy in copies:
            copy.start()
        return copies

    def sum_of(buffer, copies):
        for copy in copies:
            copy.wait_recv()
        summed = buffer[0]
        for slot in range(1, buffer.shape[0]):
            summed = summed + buffer[slot]
        return summed

    near_slot = own_cut * inner + ii
    sources = [grams.at[q] for q in range(cuts) for r in range(inner) if q or r]
    near_copies = exchange(near, near_slot, near_ids, sources, ns, nr)
    near[near_slot] = grams[0]
    summed = sum_of(near, near_copies)
    far[oi] = summed
    far_copies = exchange(far, oi, far_ids, [far.at[oi]] * (outer - 1), fs, fr)
    summed = sum_of(far, far_copies) / jnp.float32(unknowns)
    for f in range(fold):
        gram_out[f * height:(f + 1) * height, :] = summed[:, f * total_cols:(f + 1) * total_cols]

    for k in range(len(SIZES)):
        @pl.when(me < slabs - 1)
        def _():
            halo(k, 1).wait_send()

        @pl.when(me > 0)
        def _():
            halo(k, 0).wait_send()

        for r in range(1, groups):
            share(k, r).wait_send()
    for copy in near_copies + far_copies:
        copy.wait_send()


def shards(block, labels, flags, stiffness, density):
    slabs, groups = lax.axis_size("slab"), lax.axis_size("vec")
    vecs, comps, _, ny, nz = block.shape
    inner = 1
    while inner * inner < slabs:
        inner *= 2
    outer = slabs // inner
    cuts = groups if ny % (8 * groups) == 0 else 1
    part_rows = ny // cuts
    total_cols = groups * vecs
    fold = max(1, 128 // total_cols)
    terms = (vecs // fold, fold * total_cols)
    flat_block = block.reshape(vecs, comps, ny, nz)
    bf16, f32, vmem = jnp.bfloat16, jnp.float32, pltpu.VMEM
    dma = pltpu.SemaphoreType.DMA
    steps = len(SIZES)
    anywhere = pl.BlockSpec(memory_space=pl.ANY)
    filtered, gram = pl.pallas_call(
        functools.partial(kernel, slabs, groups, inner, comps * slabs * ny * nz),
        out_shape=(vmem((vecs, comps, ny, nz), bf16), vmem((vecs, total_cols), f32)),
        in_specs=[anywhere] * 5,
        out_specs=(pl.BlockSpec(memory_space=vmem), pl.BlockSpec(memory_space=vmem)),
        scratch_shapes=[
            vmem((vecs, comps, ny, nz), bf16),
            vmem((ny, nz), jnp.int32),
            vmem((ny, nz), jnp.int32),
            pltpu.SMEM(stiffness.shape, f32),
            pltpu.SMEM(density.shape, f32),
            vmem((3, vecs, comps, ny, nz), bf16),
            vmem((3, 3 * nz, 4 * nz), bf16),
            vmem((cuts, vecs, comps, part_rows, nz), bf16),
            vmem((groups - 1, vecs, comps, part_rows, nz), bf16),
            vmem((cuts, vecs, comps, part_rows, nz), bf16),
            vmem((cuts, groups, vecs, vecs * part_rows), f32),
            vmem((cuts,) + terms, f32),
            vmem((cuts * inner,) + terms, f32),
            vmem((outer,) + terms, f32),
            dma((5,)),
            dma((2, steps)),
            dma((2, steps)),
            dma((groups - 1, steps)),
            dma((groups - 1, steps)),
            dma((cuts * inner - 1,)),
            dma((cuts * inner - 1,)),
            dma((outer - 1,)),
            dma((outer - 1,)),
        ],
        compiler_params=pltpu.CompilerParams(collective_id=0, has_side_effects=True),
        name="stiffness_gram",
    )(flat_block, labels, flags, stiffness, density)
    return filtered.reshape(block.shape), gram


def solution(mesh):
    in_specs = (
        P("vec", None, "slab", None, None),
        P("slab", None, None),
        P("slab", None, None),
        P(),
        P(),
    )
    out_specs = (P("vec", None, "slab", None, None), P("vec", None))
    return jax.shard_map(shards, mesh=mesh, in_specs=in_specs, out_specs=out_specs, check_vma=False)
```

time: 33.6 us -> 31 us (0.923)
  Pallas kernels: 30.3 us -> 28.8 us
  local copies, waits for them, and re-layouts: 2.38 us -> 1.35 us
    pallas_call x1, Pallas kernels: 30.3 us -> 28.8 us  [shards(): pl.pallas_call(functools.partial(kernel, slabs, groups, inner, comps * sl...]
    unnamed x4 -> x2, local copies, waits for them, and re-layouts: 2.38 us -> 1.35 us
where the time goes in v2:
time: 31 us; the launch traced here: 30.8 us
  Pallas kernels  28.8 us (93%)
  local copies, waits for them, and re-layouts  1.35 us (4%)
  between operations  0.64 us (2%)
    pallas_call x1, Pallas kernels, shards(): pl.pallas_call(functools.partial(kernel, slabs, groups, inner, comps * sl...  28.8 us
    unnamed x2, local copies, waits for them, and re-layouts  1.35 us

profile of v2, /device:TPU:0, one launch (start us, length us, event | category | flops | bytes accessed | tf_op | source)
XLA Modules:
  0.0 30.8 jit_solution(13692049261514642712)
XLA Ops:
  0.6 28.8 %stiffness_gram.1 = (bf16[32,3,16,128]{3,2,1,0:T(8,128)(2,1)S(1)}, f32[32,64]{1,0:T(8,128)S(1)}) custom-call(bf16[32,3,16,128]{3,2,1,0:T(8,128)(2,1)} %bitcast.5, s32[1,16,128]{2,1,0:T(8,128)} %labels_hbm.1, s32[1,16,128]{2,1,0:T(8,128)} %flags_hbm.1, f32[4]{0:T(128)} %stiff_hbm.1, f32[4]{0:T(128)} %dens_hbm.1), custom_call_target="tpu_custom_call" | custom-call | tf_op jit(solution)/shard_map/stiffness_gram/pallas_call | solution.py:346
  29.5 0.7 %copy.10 = bf16[32,3,1,16,128]{4,3,2,1,0:T(8,128)(2,1)} copy(bf16[32,3,1,16,128]{4,3,2,1,0:T(8,128)(2,1)S(1)} %bitcast.4) | data formatting | bytes 786432
  30.2 0.6 %copy.11 = f32[32,64]{1,0:T(8,128)} copy(f32[32,64]{1,0:T(8,128)S(1)} %get-tuple-element.9) | data formatting | bytes 16384

commit v3 on v2

--- a/solution.py
+++ b/solution.py
@@ -8,7 +8,7 @@
 from jax.sharding import PartitionSpec as P
 
 MESH = pl.DeviceIdType.MESH
-SIZES = (8, 8, 8, 4, 4)
+SIZES = (8, 16, 8)
 UNIT = 8
 
 A = (1, 4, 1)
@@ -203,8 +203,8 @@
             arrived(k, r).wait_recv()
             if cuts > 1:
                 weigh(r, starts[k], SIZES[k])
-            if (starts[k] + SIZES[k]) % UNIT == 0:
-                corner(r, starts[k] // UNIT)
+            for unit in range(starts[k] // UNIT, (starts[k] + SIZES[k]) // UNIT):
+                corner(r, unit)
 
     for k, size in enumerate(SIZES):
         part = parts[k]
@@ -247,8 +247,8 @@
         for r in range(1, groups):
             share(k, r).start()
         weigh(0, starts[k], size)
-        if (starts[k] + size) % UNIT == 0:
-            corner(0, starts[k] // UNIT)
+        for unit in range(starts[k] // UNIT, (starts[k] + size) // UNIT):
+            corner(0, unit)
         if k > 0:
             others(k - 1)
     others(len(SIZES) - 1)

time: 31 us -> 29.4 us (0.948)
  Pallas kernels: 28.8 us -> 27.2 us
    pallas_call x1, Pallas kernels: 28.8 us -> 27.2 us  [shards(): pl.pallas_call(functools.partial(kernel, slabs, groups, inner, comps * sl...]
where the time goes in v3:
time: 29.4 us; the launch traced here: 29.2 us
  Pallas kernels  27.2 us (93%)
  local copies, waits for them, and re-layouts  1.35 us (5%)
  between operations  0.64 us (2%)
    pallas_call x1, Pallas kernels, shards(): pl.pallas_call(functools.partial(kernel, slabs, groups, inner, comps * sl...  27.2 us
    unnamed x2, local copies, waits for them, and re-layouts  1.35 us

profile of v3, /device:TPU:0, one launch (start us, length us, event | category | flops | bytes accessed | tf_op | source)
XLA Modules:
  0.0 29.2 jit_solution(12901181180318407891)
XLA Ops:
  0.6 27.2 %stiffness_gram.1 = (bf16[32,3,16,128]{3,2,1,0:T(8,128)(2,1)S(1)}, f32[32,64]{1,0:T(8,128)S(1)}) custom-call(bf16[32,3,16,128]{3,2,1,0:T(8,128)(2,1)} %bitcast.5, s32[1,16,128]{2,1,0:T(8,128)} %labels_hbm.1, s32[1,16,128]{2,1,0:T(8,128)} %flags_hbm.1, f32[4]{0:T(128)} %stiff_hbm.1, f32[4]{0:T(128)} %dens_hbm.1), custom_call_target="tpu_custom_call" | custom-call | tf_op jit(solution)/shard_map/stiffness_gram/pallas_call | solution.py:346
  27.8 0.7 %copy.10 = bf16[32,3,1,16,128]{4,3,2,1,0:T(8,128)(2,1)} copy(bf16[32,3,1,16,128]{4,3,2,1,0:T(8,128)(2,1)S(1)} %bitcast.4) | data formatting | bytes 786432
  28.6 0.6 %copy.11 = f32[32,64]{1,0:T(8,128)} copy(f32[32,64]{1,0:T(8,128)S(1)} %get-tuple-element.9) | data formatting | bytes 16384
